TPU v7x, 32 devices: a whole 2x2x4 slice. The times are simulated.
32 devices in a mesh: ens: 2 (over y), lon: 4 (over x, core), lat: 4 (over z).
Axes of the slice: x: 2, y: 2, z: 4, core: 2. Of those that a mesh axis runs over, the one named last changes fastest.
Arguments:
- noise: float32 [64, 64, 512], P('ens', 'lat', 'lon'), parts along dimension 0, may hold values from -6 to 6
- kappa2: float32 [32, 64, 512], P(None, 'lat', 'lon'), may hold values from 0.03 to 0.3
- conduct: float32 [3, 32, 64, 512], P(None, None, 'lat', 'lon'), may hold values from 0.3 to 3
- land: int32 [32, 64, 512], P(None, 'lat', 'lon'), may hold values 0 or 1
Outputs:
- solution_field: float32 [64, 64, 512], P('ens', 'lat', 'lon'), parts along dimension 0
- residual: float32 [64, 64, 512], P('ens', 'lat', 'lon'), parts along dimension 0
There are 2 independent parts, one for each index of `ens`. A program takes and returns all parts, laid end to end along the dimension named above; an argument that names none is the same for every part. Nothing has to cross between parts.
Inputs may be any that keep to these rules, and one draw needn't show every extreme that they name: 1 marks an ocean cell, 0 a land cell.
All inputs are finite; a program needn't handle non-finite values. No bound on the sum of `land` on one device may be relied on, other than what follows from the above.
Results may differ from a plain program's by a relative error of at most 0.00035.
Values sent between devices are 32-bit elements; how exact they have to be, the bound alone decides.
No kernel may reach another device: no remote copies, remote signals or barrier semaphores. Data moves between devices by JAX's collectives and lax.ppermute only.
A program may use at most 64 MiB of HBM per device.

v0:
```python
import math
import jax
import jax.numpy as jnp
from jax import lax
from jax.sharding import PartitionSpec as P

ITERS = 2
base_kappa = 0.001
base_conduct = 1.0


def padded_2(x, sides, width, wrap):
    for axis, dim in sides:
        size, length = (lax.axis_size(axis), x.shape[dim])
        up = [(i, (i + 1) % size) for i in range(size if wrap else size - 1)]
        down = [(j, i) for i, j in up]
        last = lax.slice_in_dim(x, length - width, length, axis=dim)
        initial = lax.slice_in_dim(x, 0, width, axis=dim)
        before = lax.ppermute(last, axis, up)
        after = lax.ppermute(initial, axis, down)
        x = jnp.concatenate([before, x, after], axis=dim)
    return x


def shifted(x, axis, by):
    size = lax.axis_size(axis)
    return lax.ppermute(x, axis, [(i, (i + by) % size) for i in range(size)])


def shifted_2(x, axis, by):
    size = lax.axis_size(axis)
    pairs = [(i, i + by) for i in range(size) if 0 <= i + by < size]
    return lax.ppermute(x, axis, pairs)


def cut_cycle(padded, width, extend):
    margin = width - extend
    return padded[:, :, margin : padded.shape[2] - margin, margin : padded.shape[3] - margin]


def divergence_form(padded, statics, width, extend):
    cycle = cut_cycle(statics, width, extend + 1)
    kappa_cells = cycle[0][:, 1:-1, 1:-1]
    east_face = cycle[2][:, 1:-1, 1:-1]
    west_face = cycle[2][:, 1:-1, :-2]
    north_face = cycle[3][:, 1:-1, 1:-1]
    south_face = cycle[3][:, :-2, 1:-1]
    upper_face = cycle[4][:, 1:-1, 1:-1]
    center = padded[:, 1:-1, 1:-1]
    zero_level = jnp.zeros_like(center[:1])
    lower_face = jnp.concatenate([zero_level, upper_face[:-1]], axis=0)
    upper_value = jnp.concatenate([center[1:], zero_level], axis=0)
    lower_value = jnp.concatenate([zero_level, center[:-1]], axis=0)
    return (
        kappa_cells * center
        + east_face * (center - padded[:, 1:-1, 2:])
        + west_face * (center - padded[:, 1:-1, :-2])
        + north_face * (center - padded[:, 2:, 1:-1])
        + south_face * (center - padded[:, :-2, 1:-1])
        + upper_face * (center - upper_value)
        + lower_face * (center - lower_value)
    )


def pad_each(field):
    across = padded_2(field, (("lon", 2),), 1, True)
    return padded_2(across, (("lat", 1),), 1, False)


def operator(field, statics, width):
    ocean = cut_cycle(statics, width, 0)[1]
    first = divergence_form(pad_each(ocean * field), statics, width, 0)
    second = divergence_form(pad_each(ocean * first), statics, width, 0)
    return ocean * second + (1.0 - ocean) * field


def spectral(block, width):
    length = block.shape[2]
    count_a = length // width
    lead = block.shape[:2]
    shaped = block.reshape(lead + (count_a, width))
    index_a = jnp.arange(count_a, dtype=jnp.int32)
    index_b = jnp.arange(width, dtype=jnp.int32)
    angle_a = (
        2.0
        * math.pi
        / count_a
        * (index_a[:, None] * index_a[None, :] % count_a).astype(jnp.float32)
    )
    angle_b = (
        2.0 * math.pi / width * (index_b[:, None] * index_b[None, :] % width).astype(jnp.float32)
    )
    angle_t = (
        2.0 * math.pi / length * (index_a[:, None] * index_b[None, :] % length).astype(jnp.float32)
    )
    cos_a, sin_a = (jnp.cos(angle_a), jnp.sin(angle_a))
    cos_b, sin_b = (jnp.cos(angle_b), jnp.sin(angle_b))
    cos_t, sin_t = (jnp.cos(angle_t), jnp.sin(angle_t))
    wave = (index_a[:, None] + count_a * index_b[None, :]).astype(jnp.float32)
    symbol = base_kappa + base_conduct * (2.0 - 2.0 * jnp.cos(2.0 * math.pi * wave / length))
    factor = 1.0 / (symbol * symbol)
    highest = lax.Precision.HIGHEST
    section_real = jnp.einsum("pqab,ak->pqkb", shaped, cos_a, precision=highest)
    section_imag = -jnp.einsum("pqab,ak->pqkb", shaped, sin_a, precision=highest)
    twist_real = section_real * cos_t + section_imag * sin_t
    twist_imag = section_imag * cos_t - section_real * sin_t
    freq_real = (
        jnp.einsum("pqkb,bm->pqkm", twist_real, cos_b, precision=highest)
        + jnp.einsum("pqkb,bm->pqkm", twist_imag, sin_b, precision=highest)
    ) * factor
    freq_imag = (
        jnp.einsum("pqkb,bm->pqkm", twist_imag, cos_b, precision=highest)
        - jnp.einsum("pqkb,bm->pqkm", twist_real, sin_b, precision=highest)
    ) * factor
    back_real = jnp.einsum("pqkm,bm->pqkb", freq_real, cos_b, precision=highest) - jnp.einsum(
        "pqkm,bm->pqkb", freq_imag, sin_b, precision=highest
    )
    back_imag = jnp.einsum("pqkm,bm->pqkb", freq_imag, cos_b, precision=highest) + jnp.einsum(
        "pqkm,bm->pqkb", freq_real, sin_b, precision=highest
    )
    turn_real = back_real * cos_t - back_imag * sin_t
    turn_imag = back_imag * cos_t + back_real * sin_t
    result = jnp.einsum("pqkb,ak->pqab", turn_real, cos_a, precision=highest) - jnp.einsum(
        "pqkb,ak->pqab", turn_imag, sin_a, precision=highest
    )
    return (result / length).reshape(block.shape)


def precondition(residual):
    width = residual.shape[2]
    turned = spectral(
        lax.all_to_all(residual, "lon", split_axis=0, concat_axis=2, tiled=True), width
    )
    return lax.all_to_all(turned, "lon", split_axis=2, concat_axis=0, tiled=True)


def paired_sums(residual, precond, image):
    return lax.psum((jnp.sum(residual * precond), jnp.sum(image * precond)), ("lon", "lat"))


def body(noise, kappa2, conduct, land):
    levels, rows, columns = noise.shape
    width = 1
    ocean = land.astype(jnp.float32)
    row_global = lax.axis_index("lat") * rows + lax.broadcasted_iota(jnp.int32, (1, rows, 1), 1)
    total_rows = rows * lax.axis_size("lat")
    north_face = jnp.where(row_global < total_rows - 1, conduct[1], 0.0)
    level_index = lax.broadcasted_iota(jnp.int32, (levels, 1, 1), 0)
    upper_face = jnp.where(level_index < levels - 1, conduct[2], 0.0)
    statics = jnp.stack([kappa2, ocean, conduct[0], north_face, upper_face])
    west_column = shifted(conduct[0][:, :, columns - 1 :], "lon", 1)
    zero_column = jnp.zeros((5, levels, rows, 1), jnp.float32)
    low_column = zero_column.at[2].set(west_column)
    statics = jnp.concatenate([low_column, statics, zero_column], axis=3)
    south_row = shifted_2(statics[3][:, rows - 1 :, :], "lat", 1)
    zero_row = jnp.zeros((5, levels, 1, columns + 2), jnp.float32)
    low_row = zero_row.at[3].set(south_row)
    statics = jnp.concatenate([low_row, statics, zero_row], axis=2)
    solution = jnp.zeros_like(noise)
    residual = noise
    precond = precondition(residual)
    image = operator(precond, statics, width)
    energy, curvature = paired_sums(residual, precond, image)
    alpha = energy / curvature
    direction, along = (precond, image)
    for iteration in range(ITERS):
        solution = solution + alpha * direction
        residual = residual - alpha * along
        if iteration < ITERS - 1:
            precond = precondition(residual)
            image = operator(precond, statics, width)
            renewed, curvature = paired_sums(residual, precond, image)
            ratio = renewed / energy
            alpha = renewed / (curvature - ratio * renewed / alpha)
            direction = precond + ratio * direction
            along = image + ratio * along
            energy = renewed
    return (solution, residual)


def solution(mesh):
    return jax.shard_map(
        body,
        mesh=mesh,
        in_specs=(
            P("ens", "lat", "lon"),
            P(None, "lat", "lon"),
            P(None, None, "lat", "lon"),
            P(None, "lat", "lon"),
        ),
        out_specs=(P("ens", "lat", "lon"), P("ens", "lat", "lon")),
        check_vma=False,
    )
```

profile of v0, /device:TPU:0, one launch (start us, length us, event | category | flops | bytes accessed | tf_op | source)
XLA Modules:
  0.0 230.5 jit_solution(14411306132536024307)
XLA Ops:
  0.6 4.4 %all-to-all-start = ((f32[32,16,128]{2,1,0:T(8,128)}), f32[32,16,128]{2,1,0:T(8,128)S(1)}, u32[]{:S(2)}, u32[]{:S(2)}) async-start(f32[32,16,128]{2,1,0:T(8,128)} %param.8), calls=%async_computation | async-start | bytes 524288 | tf_op jit(solution)/shard_map/all_to_all | solution.py:132
  8.1 5.7 %collective-permute-done = f32[32,16,1]{2,1,0:T(8,128)S(1)} collective-permute-done((f32[32,16,1]{2,1,0:T(8,128)S(1)}, f32[32,16,1]{2,1,0:T(8,128)S(1)}, u32[]{:S(2)}, u32[]{:S(2)}) %collective-permute-start) | collective-permute-done | bytes 2080 | tf_op jit(solution)/shard_map/ppermute | solution.py:27
  15.9 4.1 %collective-permute-start.1 = (f32[32,1,130]{2,1,0:T(1,128)S(1)}, f32[32,1,130]{2,1,0:T(1,128)S(1)}, u32[]{:S(2)}, u32[]{:S(2)}) collective-permute-start(f32[32,1,130]{2,1,0:T(1,128)S(1)} %slice.336), channel_id=1, source_target_pairs={{0,1},{1,2},{2,3},{4,5},{5,6},{6,7},{8,9},{9,10},{10,11},{12,13},{... | collective-permute-start | bytes 49928 | tf_op jit(solution)/shard_map/ppermute | solution.py:33
  28.1 2.0 copy.133
  30.1 2.9 %reshape.184 = f32[4,1,16384]{2,1,0:T(1,128)} reshape(f32[512,8,16]{2,1,0:T(8,128)} %bitcast.172) | data formatting | bytes 524288
  33.0 3.6 %all-to-all-start.1 = ((f32[4,1,16384]{2,1,0:T(1,128)}), f32[4,1,16384]{2,1,0:T(1,128)S(1)}, u32[]{:S(2)}, u32[]{:S(2)}) async-start(f32[4,1,16384]{2,1,0:T(1,128)} %reshape.184), calls=%async_computation.1 | async-start | bytes 524288 | tf_op jit(solution)/shard_map/all_to_all | solution.py:134
  36.6 4.8 %fusion = f32[5,32,18,130]{3,2,1,0:T(8,128)} fusion(f32[1,32,1,130]{3,2,1,0:T(1,128)S(1)} %bitcast.182, f32[5,32,16,1]{3,2,1,0:T(8,128)S(1)} %broadcast_in_dim.29, f32[5,32,16,128]{3,2,1,0:T(8,128)} %copy-done.1, f32[5,32,16,1]{3,2,1,0:T(8,128)S(1)} %scatter.6, f32[18]{0:T(128)S(1)} %pad.79.clone), kind=kLoop, calls=%fused_computation.1 | loop fusion | flops 2246400 | bytes 2845512 | tf_op jit(solution)/shard_map/concatenate | solution.py:158
  46.1 1.7 collective-permute-start.2
  47.8 2.2 slice_bitcast_fusion.3
  50.1 3.4 %collective-permute-done.3 = f32[32,16,1]{2,1,0:T(8,128)S(1)} collective-permute-done((f32[32,16,1]{2,1,0:T(8,128)S(1)}, f32[32,16,1]{2,1,0:T(8,128)S(1)}, u32[]{:S(2)}, u32[]{:S(2)}) %collective-permute-start.3) | collective-permute-done | bytes 2080 | tf_op jit(solution)/shard_map/ppermute | solution.py:19
  55.1 4.5 %collective-permute-start.5 = (f32[32,1,130]{2,1,0:T(1,128)S(1)}, f32[32,1,130]{2,1,0:T(1,128)S(1)}, u32[]{:S(2)}, u32[]{:S(2)}) collective-permute-start(f32[32,1,130]{2,1,0:T(1,128)S(1)} %get-tuple-element.51), channel_id=1, source_target_pairs={{0,1},{1,2},{2,3},{4,5},{5,6},{6,7},{8,9},{9,10},{10,11},{12,13},{... | collective-permute-start | bytes 49928 | tf_op jit(solution)/shard_map/ppermute | solution.py:19
  62.3 1.7 collective-permute-start.6
  64.1 5.8 %collective-permute-done.7 = f32[32,16,1]{2,1,0:T(8,128)S(1)} collective-permute-done((f32[32,16,1]{2,1,0:T(8,128)S(1)}, f32[32,16,1]{2,1,0:T(8,128)S(1)}, u32[]{:S(2)}, u32[]{:S(2)}) %collective-permute-start.7) | collective-permute-done | bytes 2080 | tf_op jit(solution)/shard_map/ppermute | solution.py:19
  71.5 4.8 %collective-permute-start.9 = (f32[32,1,130]{2,1,0:T(1,128)S(1)}, f32[32,1,130]{2,1,0:T(1,128)S(1)}, u32[]{:S(2)}, u32[]{:S(2)}) collective-permute-start(f32[32,1,130]{2,1,0:T(1,128)S(1)} %get-tuple-element.47), channel_id=1, source_target_pairs={{0,1},{1,2},{2,3},{4,5},{5,6},{6,7},{8,9},{9,10},{10,11},{12,13},{... | collective-permute-start | bytes 49928 | tf_op jit(solution)/shard_map/ppermute | solution.py:19
  76.3 1.7 collective-permute-done.9
  79.5 34.8 %all-reduce.12 = (f32[]{:T(128)}, f32[]{:T(128)}) all-reduce(f32[]{:T(128)} %get-tuple-element.31, f32[]{:T(128)} %get-tuple-element.30), channel_id=1, replica_groups=mesh['ens'=2,'lon'=4,'lat'=4] {'lon','lat'}, use_global_device_ids=true, to_apply=%region_1.2 | all-reduce | flops 2 | bytes 16 | tf_op jit(solution)/shard_map/psum | solution.py:138
  117.4 8.4 %all_to_all.66 = f32[32,16,128]{2,1,0:T(8,128)S(1)} all-to-all(f32[32,16,128]{2,1,0:T(8,128)S(1)} %multiply_subtract_fusion.2), channel_id=1, replica_groups=mesh['ens'=2,'lon'=4,'lat'=4] {'lon'}, dimensions={0} | all-to-all | bytes 524288 | tf_op jit(solution)/shard_map/all_to_all | solution.py:132
  133.9 2.0 copy.137
  135.8 2.3 reshape.186
  138.1 9.1 %all_to_all.67 = f32[4,1,16384]{2,1,0:T(1,128)} all-to-all(f32[4,1,16384]{2,1,0:T(1,128)S(1)} %reshape.186), channel_id=1, replica_groups=mesh['ens'=2,'lon'=4,'lat'=4] {'lon'}, dimensions={0} | all-to-all | bytes 524288 | tf_op jit(solution)/shard_map/all_to_all | solution.py:134
  147.2 2.3 reduce.5
  149.5 2.0 reshape.187
  151.5 2.9 %copy.138 = f32[8,16,4,128]{3,2,1,0:T(4,128)} copy(f32[8,16,4,128]{1,0,3,2:T(8,128)} %bitcast.175) | data formatting | bytes 524288 | tf_op jit(solution)/shard_map/all_to_all | solution.py:134
  155.6 1.7 collective-permute-start.10
  157.3 6.2 %collective-permute-done.11 = f32[32,16,1]{2,1,0:T(8,128)S(1)} collective-permute-done((f32[32,16,1]{2,1,0:T(8,128)S(1)}, f32[32,16,1]{2,1,0:T(8,128)S(1)}, u32[]{:S(2)}, u32[]{:S(2)}) %collective-permute-start.11) | collective-permute-done | bytes 2080 | tf_op jit(solution)/shard_map/ppermute | solution.py:19
  165.1 4.5 %collective-permute-start.13 = (f32[32,1,130]{2,1,0:T(1,128)S(1)}, f32[32,1,130]{2,1,0:T(1,128)S(1)}, u32[]{:S(2)}, u32[]{:S(2)}) collective-permute-start(f32[32,1,130]{2,1,0:T(1,128)S(1)} %get-tuple-element.45), channel_id=1, source_target_pairs={{0,1},{1,2},{2,3},{4,5},{5,6},{6,7},{8,9},{9,10},{10,11},{12,13},{... | collective-permute-start | bytes 49928 | tf_op jit(solution)/shard_map/ppermute | solution.py:19
  172.3 1.7 collective-permute-start.14
  174.0 6.3 %collective-permute-done.15 = f32[32,16,1]{2,1,0:T(8,128)S(1)} collective-permute-done((f32[32,16,1]{2,1,0:T(8,128)S(1)}, f32[32,16,1]{2,1,0:T(8,128)S(1)}, u32[]{:S(2)}, u32[]{:S(2)}) %collective-permute-start.15) | collective-permute-done | bytes 2080 | tf_op jit(solution)/shard_map/ppermute | solution.py:19
  181.9 4.9 %collective-permute-start.17 = (f32[32,1,130]{2,1,0:T(1,128)S(1)}, f32[32,1,130]{2,1,0:T(1,128)S(1)}, u32[]{:S(2)}, u32[]{:S(2)}) collective-permute-start(f32[32,1,130]{2,1,0:T(1,128)S(1)} %get-tuple-element.43), channel_id=1, source_target_pairs={{0,1},{1,2},{2,3},{4,5},{5,6},{6,7},{8,9},{9,10},{10,11},{12,13},{... | collective-permute-start | bytes 49928 | tf_op jit(solution)/shard_map/ppermute | solution.py:19
  188.4 2.3 fusion.73
  190.6 32.7 %all-reduce.11 = (f32[]{:T(128)}, f32[]{:T(128)}) all-reduce(f32[]{:T(128)} %get-tuple-element.29, f32[]{:T(128)} %get-tuple-element.28), channel_id=1, replica_groups=mesh['ens'=2,'lon'=4,'lat'=4] {'lon','lat'}, use_global_device_ids=true, to_apply=%region_5.6 | all-reduce | flops 2 | bytes 16 | tf_op jit(solution)/shard_map/psum | solution.py:138
  228.7 1.9 multiply_subtract_fusion
  (111 shorter events, 44.0 us)
Async XLA Ops:
  0.6 6.3 %copy-start.9 = (f32[3,32,16,128]{3,2,1,0:T(8,128)S(1)}, f32[3,32,16,128]{3,2,1,0:T(8,128)}, u32[]{:S(2)}) copy-start(f32[3,32,16,128]{3,2,1,0:T(8,128)} %param.10) | copy-start | bytes 2359300
  0.6 19.3 %all-to-all-start = ((f32[32,16,128]{2,1,0:T(8,128)}), f32[32,16,128]{2,1,0:T(8,128)S(1)}, u32[]{:S(2)}, u32[]{:S(2)}) async-start(f32[32,16,128]{2,1,0:T(8,128)} %param.8), calls=%async_computation | async-start | bytes 524288 | tf_op jit(solution)/shard_map/all_to_all | solution.py:132
  7.2 6.7 %collective-permute-start = (f32[32,16,1]{2,1,0:T(8,128)S(1)}, f32[32,16,1]{2,1,0:T(8,128)S(1)}, u32[]{:S(2)}, u32[]{:S(2)}) collective-permute-start(f32[32,16,1]{2,1,0:T(8,128)S(1)} %slice.335), channel_id=1, source_target_pairs={{0,4},{4,8},{8,12},{12,0},{1,5},{5,9},{9,13},{13,1},{2,6},{6,10},{... | collective-permute-start | bytes 6152 | tf_op jit(solution)/shard_map/ppermute | solution.py:27
  8.0 6.0 %copy-start.1 = (f32[5,32,16,128]{3,2,1,0:T(8,128)}, f32[5,32,16,128]{3,2,1,0:T(8,128)S(1)}, u32[]{:S(2)}) copy-start(f32[5,32,16,128]{3,2,1,0:T(8,128)S(1)} %select_dynamic-update-slice_fusion) | copy-start | bytes 3932164
  14.2 1.3 copy-start.2
  15.9 20.7 %collective-permute-start.1 = (f32[32,1,130]{2,1,0:T(1,128)S(1)}, f32[32,1,130]{2,1,0:T(1,128)S(1)}, u32[]{:S(2)}, u32[]{:S(2)}) collective-permute-start(f32[32,1,130]{2,1,0:T(1,128)S(1)} %slice.336), channel_id=1, source_target_pairs={{0,1},{1,2},{2,3},{4,5},{5,6},{6,7},{8,9},{9,10},{10,11},{12,13},{... | collective-permute-start | bytes 49928 | tf_op jit(solution)/shard_map/ppermute | solution.py:33
  33.0 9.4 %all-to-all-start.1 = ((f32[4,1,16384]{2,1,0:T(1,128)}), f32[4,1,16384]{2,1,0:T(1,128)S(1)}, u32[]{:S(2)}, u32[]{:S(2)}) async-start(f32[4,1,16384]{2,1,0:T(1,128)} %reshape.184), calls=%async_computation.1 | async-start | bytes 524288 | tf_op jit(solution)/shard_map/all_to_all | solution.py:134
  44.9 1.0 copy-start
  46.0 7.5 %collective-permute-start.3 = (f32[32,16,1]{2,1,0:T(8,128)S(1)}, f32[32,16,1]{2,1,0:T(8,128)S(1)}, u32[]{:S(2)}, u32[]{:S(2)}) collective-permute-start(f32[32,16,1]{2,1,0:T(8,128)S(1)} %get-tuple-element.74), channel_id=1, source_target_pairs={{0,4},{4,8},{8,12},{12,0},{1,5},{5,9},{9,13},{13,1},{2,6},{6,10},{... | collective-permute-start | bytes 6152 | tf_op jit(solution)/shard_map/ppermute | solution.py:19
  46.1 7.4 %collective-permute-start.2 = (f32[32,16,1]{2,1,0:T(8,128)S(1)}, f32[32,16,1]{2,1,0:T(8,128)S(1)}, u32[]{:S(2)}, u32[]{:S(2)}) collective-permute-start(f32[32,16,1]{2,1,0:T(8,128)S(1)} %get-tuple-element.75), channel_id=1, source_target_pairs={{4,0},{8,4},{12,8},{0,12},{5,1},{9,5},{13,9},{1,13},{6,2},{10,6},{... | collective-permute-start | bytes 6152 | tf_op jit(solution)/shard_map/ppermute | solution.py:20
  50.0 28.0 %copy-start.3 = (f32[32,18,130]{2,1,0:T(8,128)}, f32[32,18,130]{2,1,0:T(8,128)S(1)}, u32[]{:S(2)}) copy-start(f32[32,18,130]{2,1,0:T(8,128)S(1)} %get-tuple-element.38) | copy-start | bytes 898564
  53.8 6.2 %collective-permute-start.4 = (f32[32,1,130]{2,1,0:T(1,128)S(1)}, f32[32,1,130]{2,1,0:T(1,128)S(1)}, u32[]{:S(2)}, u32[]{:S(2)}) collective-permute-start(f32[32,1,130]{2,1,0:T(1,128)S(1)} %get-tuple-element.50), channel_id=1, source_target_pairs={{1,0},{2,1},{3,2},{5,4},{6,5},{7,6},{9,8},{10,9},{11,10},{13,12},{... | collective-permute-start | bytes 49928 | tf_op jit(solution)/shard_map/ppermute | solution.py:20
  55.1 6.1 %collective-permute-start.5 = (f32[32,1,130]{2,1,0:T(1,128)S(1)}, f32[32,1,130]{2,1,0:T(1,128)S(1)}, u32[]{:S(2)}, u32[]{:S(2)}) collective-permute-start(f32[32,1,130]{2,1,0:T(1,128)S(1)} %get-tuple-element.51), channel_id=1, source_target_pairs={{0,1},{1,2},{2,3},{4,5},{5,6},{6,7},{8,9},{9,10},{10,11},{12,13},{... | collective-permute-start | bytes 49928 | tf_op jit(solution)/shard_map/ppermute | solution.py:19
  62.1 15.9 %copy-start.8 = (f32[32,16,128]{2,1,0:T(8,128)S(1)}, f32[32,16,128]{2,1,0:T(8,128)}, u32[]{:S(2)}) copy-start(f32[32,16,128]{2,1,0:T(8,128)} %param.8) | copy-start | bytes 786436
  62.3 7.6 %collective-permute-start.7 = (f32[32,16,1]{2,1,0:T(8,128)S(1)}, f32[32,16,1]{2,1,0:T(8,128)S(1)}, u32[]{:S(2)}, u32[]{:S(2)}) collective-permute-start(f32[32,16,1]{2,1,0:T(8,128)S(1)} %get-tuple-element.68), channel_id=1, source_target_pairs={{0,4},{4,8},{8,12},{12,0},{1,5},{5,9},{9,13},{13,1},{2,6},{6,10},{... | collective-permute-start | bytes 6152 | tf_op jit(solution)/shard_map/ppermute | solution.py:19
  62.3 7.6 %collective-permute-start.6 = (f32[32,16,1]{2,1,0:T(8,128)S(1)}, f32[32,16,1]{2,1,0:T(8,128)S(1)}, u32[]{:S(2)}, u32[]{:S(2)}) collective-permute-start(f32[32,16,1]{2,1,0:T(8,128)S(1)} %get-tuple-element.69), channel_id=1, source_target_pairs={{4,0},{8,4},{12,8},{0,12},{5,1},{9,5},{13,9},{1,13},{6,2},{10,6},{... | collective-permute-start | bytes 6152 | tf_op jit(solution)/shard_map/ppermute | solution.py:20
  70.2 6.2 %collective-permute-start.8 = (f32[32,1,130]{2,1,0:T(1,128)S(1)}, f32[32,1,130]{2,1,0:T(1,128)S(1)}, u32[]{:S(2)}, u32[]{:S(2)}) collective-permute-start(f32[32,1,130]{2,1,0:T(1,128)S(1)} %get-tuple-element.46), channel_id=1, source_target_pairs={{1,0},{2,1},{3,2},{5,4},{6,5},{7,6},{9,8},{10,9},{11,10},{13,12},{... | collective-permute-start | bytes 49928 | tf_op jit(solution)/shard_map/ppermute | solution.py:20
  71.5 6.6 %collective-permute-start.9 = (f32[32,1,130]{2,1,0:T(1,128)S(1)}, f32[32,1,130]{2,1,0:T(1,128)S(1)}, u32[]{:S(2)}, u32[]{:S(2)}) collective-permute-start(f32[32,1,130]{2,1,0:T(1,128)S(1)} %get-tuple-element.47), channel_id=1, source_target_pairs={{0,1},{1,2},{2,3},{4,5},{5,6},{6,7},{8,9},{9,10},{10,11},{12,13},{... | collective-permute-start | bytes 49928 | tf_op jit(solution)/shard_map/ppermute | solution.py:19
  79.5 48.0 %copy-start.7 = (f32[32,16,128]{2,1,0:T(8,128)}, f32[32,16,128]{2,1,0:T(8,128)S(1)}, u32[]{:S(2)}) copy-start(f32[32,16,128]{2,1,0:T(8,128)S(1)} %get-tuple-element.37) | copy-start | bytes 786436
  116.7 0.7 copy-start.5
  155.4 15.8 %copy-start.4 = (f32[32,18,130]{2,1,0:T(8,128)S(1)}, f32[32,18,130]{2,1,0:T(8,128)}, u32[]{:S(2)}) copy-start(f32[32,18,130]{2,1,0:T(8,128)} %copy-done.3) | copy-start | bytes 898564
  155.5 8.0 %collective-permute-start.11 = (f32[32,16,1]{2,1,0:T(8,128)S(1)}, f32[32,16,1]{2,1,0:T(8,128)S(1)}, u32[]{:S(2)}, u32[]{:S(2)}) collective-permute-start(f32[32,16,1]{2,1,0:T(8,128)S(1)} %get-tuple-element.66), channel_id=1, source_target_pairs={{0,4},{4,8},{8,12},{12,0},{1,5},{5,9},{9,13},{13,1},{2,6},{6,10},{... | collective-permute-start | bytes 6152 | tf_op jit(solution)/shard_map/ppermute | solution.py:19
  155.6 7.9 %collective-permute-start.10 = (f32[32,16,1]{2,1,0:T(8,128)S(1)}, f32[32,16,1]{2,1,0:T(8,128)S(1)}, u32[]{:S(2)}, u32[]{:S(2)}) collective-permute-start(f32[32,16,1]{2,1,0:T(8,128)S(1)} %get-tuple-element.67), channel_id=1, source_target_pairs={{4,0},{8,4},{12,8},{0,12},{5,1},{9,5},{13,9},{1,13},{6,2},{10,6},{... | collective-permute-start | bytes 6152 | tf_op jit(solution)/shard_map/ppermute | solution.py:20
  163.8 5.9 %collective-permute-start.12 = (f32[32,1,130]{2,1,0:T(1,128)S(1)}, f32[32,1,130]{2,1,0:T(1,128)S(1)}, u32[]{:S(2)}, u32[]{:S(2)}) collective-permute-start(f32[32,1,130]{2,1,0:T(1,128)S(1)} %get-tuple-element.44), channel_id=1, source_target_pairs={{1,0},{2,1},{3,2},{5,4},{6,5},{7,6},{9,8},{10,9},{11,10},{13,12},{... | collective-permute-start | bytes 49928 | tf_op jit(solution)/shard_map/ppermute | solution.py:20
  165.1 6.1 %collective-permute-start.13 = (f32[32,1,130]{2,1,0:T(1,128)S(1)}, f32[32,1,130]{2,1,0:T(1,128)S(1)}, u32[]{:S(2)}, u32[]{:S(2)}) collective-permute-start(f32[32,1,130]{2,1,0:T(1,128)S(1)} %get-tuple-element.45), channel_id=1, source_target_pairs={{0,1},{1,2},{2,3},{4,5},{5,6},{6,7},{8,9},{9,10},{10,11},{12,13},{... | collective-permute-start | bytes 49928 | tf_op jit(solution)/shard_map/ppermute | solution.py:19
  172.1 16.3 %copy-start.6 = (f32[32,16,128]{2,1,0:T(8,128)S(1)}, f32[32,16,128]{2,1,0:T(8,128)}, u32[]{:S(2)}) copy-start(f32[32,16,128]{2,1,0:T(8,128)} %copy-done.5) | copy-start | bytes 786436
  172.2 8.1 %collective-permute-start.15 = (f32[32,16,1]{2,1,0:T(8,128)S(1)}, f32[32,16,1]{2,1,0:T(8,128)S(1)}, u32[]{:S(2)}, u32[]{:S(2)}) collective-permute-start(f32[32,16,1]{2,1,0:T(8,128)S(1)} %get-tuple-element.60), channel_id=1, source_target_pairs={{0,4},{4,8},{8,12},{12,0},{1,5},{5,9},{9,13},{13,1},{2,6},{6,10},{... | collective-permute-start | bytes 6152 | tf_op jit(solution)/shard_map/ppermute | solution.py:19
  172.3 8.1 %collective-permute-start.14 = (f32[32,16,1]{2,1,0:T(8,128)S(1)}, f32[32,16,1]{2,1,0:T(8,128)S(1)}, u32[]{:S(2)}, u32[]{:S(2)}) collective-permute-start(f32[32,16,1]{2,1,0:T(8,128)S(1)} %get-tuple-element.61), channel_id=1, source_target_pairs={{4,0},{8,4},{12,8},{0,12},{5,1},{9,5},{13,9},{1,13},{6,2},{10,6},{... | collective-permute-start | bytes 6152 | tf_op jit(solution)/shard_map/ppermute | solution.py:20
  180.6 6.2 %collective-permute-start.16 = (f32[32,1,130]{2,1,0:T(1,128)S(1)}, f32[32,1,130]{2,1,0:T(1,128)S(1)}, u32[]{:S(2)}, u32[]{:S(2)}) collective-permute-start(f32[32,1,130]{2,1,0:T(1,128)S(1)} %get-tuple-element.42), channel_id=1, source_target_pairs={{1,0},{2,1},{3,2},{5,4},{6,5},{7,6},{9,8},{10,9},{11,10},{13,12},{... | collective-permute-start | bytes 49928 | tf_op jit(solution)/shard_map/ppermute | solution.py:20
  181.9 6.4 %collective-permute-start.17 = (f32[32,1,130]{2,1,0:T(1,128)S(1)}, f32[32,1,130]{2,1,0:T(1,128)S(1)}, u32[]{:S(2)}, u32[]{:S(2)}) collective-permute-start(f32[32,1,130]{2,1,0:T(1,128)S(1)} %get-tuple-element.43), channel_id=1, source_target_pairs={{0,1},{1,2},{2,3},{4,5},{5,6},{6,7},{8,9},{9,10},{10,11},{12,13},{... | collective-permute-start | bytes 49928 | tf_op jit(solution)/shard_map/ppermute | solution.py:19
where the time goes:
time: 232 us; the launch traced here: 231 us
  blocking collectives  84.9 us (37%)
  starting transfers between devices  43.7 us (19%)
  waiting for transfers between devices  34.7 us (15%)
  local copies, waits for them, and re-layouts  23.7 us (10%)
  other arithmetic  20.2 us (9%)
  matrix products  16 us (7%)
  between operations  7.26 us (3%)
    psum x2, blocking collectives, paired_sums(): lax.psum((jnp.sum(residual * precond), jnp.sum(image * precond)), ('lon',...  67.5 us
    ppermute x8, waiting for transfers between devices, padded_2(): before = lax.ppermute(last, axis, up)  27.8 us
    ppermute x8, starting transfers between devices, padded_2(): before = lax.ppermute(last, axis, up)  19 us
    ppermute x8, starting transfers between devices, padded_2(): after = lax.ppermute(initial, axis, down)  12.1 us
    unnamed x25, local copies, waits for them, and re-layouts  10.9 us
    all_to_all x1, blocking collectives, precondition(): lax.all_to_all(turned, 'lon', split_axis=2, concat_axis=0, tiled=True)  9.07 us
    all_to_all x1, blocking collectives, precondition(): lax.all_to_all(residual, 'lon', split_axis=0, concat_axis=2, tiled=True)  8.38 us
    ppermute x1, waiting for transfers between devices, shifted(): return lax.ppermute(x, axis, [(i, (i + by) % size) for i in range(size)])  5.71 us
  transfers between devices with their start and end apart: 20, of which 11 were waited for; matrix products, arithmetic and copies ran while one was open for 10% of the time, Pallas kernels for 0%

commit v1 on v0

--- a/solution.py
+++ b/solution.py
@@ -7,6 +7,13 @@
 ITERS = 2
 base_kappa = 0.001
 base_conduct = 1.0
+
+
+def swap_blocks(x, name, split, join):
+    count = lax.axis_size(name)
+    blocks = jnp.stack(jnp.split(x, count, axis=split), axis=0)
+    blocks = lax.all_to_all(blocks, name, split_axis=0, concat_axis=0)
+    return jnp.concatenate(blocks, axis=join)
 
 
 def padded_2(x, sides, width, wrap):
@@ -131,7 +138,7 @@
     turned = spectral(
         lax.all_to_all(residual, "lon", split_axis=0, concat_axis=2, tiled=True), width
     )
-    return lax.all_to_all(turned, "lon", split_axis=2, concat_axis=0, tiled=True)
+    return swap_blocks(turned, "lon", 2, 0)
 
 
 def paired_sums(residual, precond, image):

time: 232 us -> 213 us (0.918)
  local copies, waits for them, and re-layouts: 23.7 us -> 8.93 us
  other arithmetic: 20.2 us -> 17.5 us
    unnamed x25, local copies, waits for them, and re-layouts: 10.9 us -> 3.26 us
    all_to_all x5 -> x0, local copies, waits for them, and re-layouts: 5.07 us -> none  [precondition(): lax.all_to_all(turned, 'lon', split_axis=2, concat_axis=0, tiled=True)]
    all_to_all x2 -> x0, other arithmetic: 3.65 us -> none  [precondition(): lax.all_to_all(turned, 'lon', split_axis=2, concat_axis=0, tiled=True)]
    reshape x2, local copies, waits for them, and re-layouts: 3.93 us -> 0.91 us  [spectral(): return (result / length).reshape(block.shape)]
  transfers between devices with their start and end apart: 20 -> 20, of which waited for: 11 -> 11; matrix products, arithmetic and copies ran while one was open for 10% -> 9% of each run, Pallas kernels for 0% -> 0%
where the time goes in v1:
time: 213 us; the launch traced here: 212 us
  blocking collectives  84.5 us (40%)
  starting transfers between devices  43.2 us (20%)
  waiting for transfers between devices  34.7 us (16%)
  other arithmetic  17.5 us (8%)
  matrix products  16 us (8%)
  local copies, waits for them, and re-layouts  8.93 us (4%)
  between operations  7.03 us (3%)
    psum x2, blocking collectives, paired_sums(): lax.psum((jnp.sum(residual * precond), jnp.sum(image * precond)), ('lon',...  67.7 us
    ppermute x8, waiting for transfers between devices, padded_2(): before = lax.ppermute(last, axis, up)  27.7 us
    ppermute x8, starting transfers between devices, padded_2(): before = lax.ppermute(last, axis, up)  19.1 us
    ppermute x8, starting transfers between devices, padded_2(): after = lax.ppermute(initial, axis, down)  11.6 us
    all_to_all x1, blocking collectives, swap_blocks(): blocks = lax.all_to_all(blocks, name, split_axis=0, concat_axis=0)  8.39 us
    all_to_all x1, blocking collectives, precondition(): lax.all_to_all(residual, 'lon', split_axis=0, concat_axis=2, tiled=True)  8.38 us
    ppermute x1, waiting for transfers between devices, shifted(): return lax.ppermute(x, axis, [(i, (i + by) % size) for i in range(size)])  5.71 us
    concatenate x1, other arithmetic, body(): statics = jnp.concatenate([low_row, statics, zero_row], axis=2)  4.86 us
  transfers between devices with their start and end apart: 20, of which 11 were waited for; matrix products, arithmetic and copies ran while one was open for 9% of the time, Pallas kernels for 0%

profile of v1, /device:TPU:0, one launch (start us, length us, event | category | flops | bytes accessed | tf_op | source)
XLA Modules:
  0.0 211.9 jit_solution(16148635258922694993)
XLA Ops:
  0.6 4.4 %all-to-all-start = ((f32[32,16,128]{2,1,0:T(8,128)}), f32[32,16,128]{2,1,0:T(8,128)S(1)}, u32[]{:S(2)}, u32[]{:S(2)}) async-start(f32[32,16,128]{2,1,0:T(8,128)} %param.8), calls=%async_computation | async-start | bytes 524288 | tf_op jit(solution)/shard_map/all_to_all | solution.py:139
  8.1 5.7 %collective-permute-done = f32[32,16,1]{2,1,0:T(8,128)S(1)} collective-permute-done((f32[32,16,1]{2,1,0:T(8,128)S(1)}, f32[32,16,1]{2,1,0:T(8,128)S(1)}, u32[]{:S(2)}, u32[]{:S(2)}) %collective-permute-start) | collective-permute-done | bytes 2080 | tf_op jit(solution)/shard_map/ppermute | solution.py:34
  15.9 4.1 %collective-permute-start.1 = (f32[32,1,130]{2,1,0:T(1,128)S(1)}, f32[32,1,130]{2,1,0:T(1,128)S(1)}, u32[]{:S(2)}, u32[]{:S(2)}) collective-permute-start(f32[32,1,130]{2,1,0:T(1,128)S(1)} %slice.336), channel_id=1, source_target_pairs={{0,1},{1,2},{2,3},{4,5},{5,6},{6,7},{8,9},{9,10},{10,11},{12,13},{... | collective-permute-start | bytes 49928 | tf_op jit(solution)/shard_map/ppermute | solution.py:40
  28.9 3.4 %all-to-all-start.1 = ((f32[4,8,16,128]{3,2,1,0:T(8,128)}), f32[4,8,16,128]{3,2,1,0:T(8,128)S(1)}, u32[]{:S(2)}, u32[]{:S(2)}) async-start(f32[4,8,16,128]{3,2,1,0:T(8,128)} %pad_maximum_fusion.34), calls=%async_computation.1 | async-start | bytes 524288 | tf_op jit(solution)/shard_map/all_to_all | solution.py:15
  32.4 4.9 %fusion = f32[5,32,18,130]{3,2,1,0:T(8,128)} fusion(f32[1,32,1,130]{3,2,1,0:T(1,128)S(1)} %bitcast.182, f32[5,32,16,1]{3,2,1,0:T(8,128)S(1)} %broadcast_in_dim.29, f32[5,32,16,128]{3,2,1,0:T(8,128)} %copy-done.1, f32[5,32,16,1]{3,2,1,0:T(8,128)S(1)} %scatter.6, f32[18]{0:T(128)S(1)} %pad.83.clone), kind=kLoop, calls=%fused_computation.1 | loop fusion | flops 2246400 | bytes 2845512 | tf_op jit(solution)/shard_map/concatenate | solution.py:165
  40.3 2.1 %slice_bitcast_fusion.3 = (f32[32,18,130]{2,1,0:T(8,128)S(1)}, f32[32,18,130]{2,1,0:T(8,128)S(1)}, f32[32,18,130]{2,1,0:T(8,128)S(1)}, f32[32,18,130]{2,1,0:T(8,128)S(1)}) fusion(f32[5,32,18,130]{3,2,1,0:T(8,128)} %fusion), kind=kLoop, calls=%fused_computation.26 | loop fusion | bytes 2396160 | tf_op jit(solution)/shard_map/squeeze | solution.py:50
  42.6 3.4 %collective-permute-done.3 = f32[32,16,1]{2,1,0:T(8,128)S(1)} collective-permute-done((f32[32,16,1]{2,1,0:T(8,128)S(1)}, f32[32,16,1]{2,1,0:T(8,128)S(1)}, u32[]{:S(2)}, u32[]{:S(2)}) %collective-permute-start.3) | collective-permute-done | bytes 2080 | tf_op jit(solution)/shard_map/ppermute | solution.py:26
  46.3 1.3 collective-permute-start.4
  47.6 4.5 %collective-permute-start.5 = (f32[32,1,130]{2,1,0:T(1,128)S(1)}, f32[32,1,130]{2,1,0:T(1,128)S(1)}, u32[]{:S(2)}, u32[]{:S(2)}) collective-permute-start(f32[32,1,130]{2,1,0:T(1,128)S(1)} %get-tuple-element.51), channel_id=1, source_target_pairs={{0,1},{1,2},{2,3},{4,5},{5,6},{6,7},{8,9},{9,10},{10,11},{12,13},{... | collective-permute-start | bytes 49928 | tf_op jit(solution)/shard_map/ppermute | solution.py:26
  52.4 1.3 collective-permute-done.5
  54.8 1.7 collective-permute-start.6
  56.6 5.7 %collective-permute-done.7 = f32[32,16,1]{2,1,0:T(8,128)S(1)} collective-permute-done((f32[32,16,1]{2,1,0:T(8,128)S(1)}, f32[32,16,1]{2,1,0:T(8,128)S(1)}, u32[]{:S(2)}, u32[]{:S(2)}) %collective-permute-start.7) | collective-permute-done | bytes 2080 | tf_op jit(solution)/shard_map/ppermute | solution.py:26
  62.6 1.3 collective-permute-start.8
  63.9 4.9 %collective-permute-start.9 = (f32[32,1,130]{2,1,0:T(1,128)S(1)}, f32[32,1,130]{2,1,0:T(1,128)S(1)}, u32[]{:S(2)}, u32[]{:S(2)}) collective-permute-start(f32[32,1,130]{2,1,0:T(1,128)S(1)} %get-tuple-element.47), channel_id=1, source_target_pairs={{0,1},{1,2},{2,3},{4,5},{5,6},{6,7},{8,9},{9,10},{10,11},{12,13},{... | collective-permute-start | bytes 49928 | tf_op jit(solution)/shard_map/ppermute | solution.py:26
  68.9 1.7 collective-permute-done.9
  70.5 1.5 fusion.80
  72.1 35.1 %all-reduce.12 = (f32[]{:T(128)}, f32[]{:T(128)}) all-reduce(f32[]{:T(128)} %get-tuple-element.31, f32[]{:T(128)} %get-tuple-element.30), channel_id=1, replica_groups=mesh['ens'=2,'lon'=4,'lat'=4] {'lon','lat'}, use_global_device_ids=true, to_apply=%region_1.2 | all-reduce | flops 2 | bytes 16 | tf_op jit(solution)/shard_map/psum | solution.py:145
  110.1 8.4 %all_to_all.40 = f32[32,16,128]{2,1,0:T(8,128)S(1)} all-to-all(f32[32,16,128]{2,1,0:T(8,128)S(1)} %multiply_subtract_fusion.2), channel_id=1, replica_groups=mesh['ens'=2,'lon'=4,'lat'=4] {'lon'}, dimensions={0} | all-to-all | bytes 524288 | tf_op jit(solution)/shard_map/all_to_all | solution.py:139
  128.5 8.4 %all_to_all.41 = f32[4,8,16,128]{3,2,1,0:T(8,128)S(1)} all-to-all(f32[4,8,16,128]{3,2,1,0:T(8,128)S(1)} %pad_maximum_fusion.35), channel_id=1, replica_groups=mesh['ens'=2,'lon'=4,'lat'=4] {'lon'}, dimensions={0} | all-to-all | bytes 524288 | tf_op jit(solution)/shard_map/all_to_all | solution.py:15
  137.1 1.7 collective-permute-start.10
  138.8 6.2 %collective-permute-done.11 = f32[32,16,1]{2,1,0:T(8,128)S(1)} collective-permute-done((f32[32,16,1]{2,1,0:T(8,128)S(1)}, f32[32,16,1]{2,1,0:T(8,128)S(1)}, u32[]{:S(2)}, u32[]{:S(2)}) %collective-permute-start.11) | collective-permute-done | bytes 2080 | tf_op jit(solution)/shard_map/ppermute | solution.py:26
  145.3 1.3 collective-permute-start.12
  146.6 4.5 %collective-permute-start.13 = (f32[32,1,130]{2,1,0:T(1,128)S(1)}, f32[32,1,130]{2,1,0:T(1,128)S(1)}, u32[]{:S(2)}, u32[]{:S(2)}) collective-permute-start(f32[32,1,130]{2,1,0:T(1,128)S(1)} %get-tuple-element.45), channel_id=1, source_target_pairs={{0,1},{1,2},{2,3},{4,5},{5,6},{6,7},{8,9},{9,10},{10,11},{12,13},{... | collective-permute-start | bytes 49928 | tf_op jit(solution)/shard_map/ppermute | solution.py:26
  151.2 1.5 collective-permute-done.13
  153.9 1.7 collective-permute-start.14
  155.6 6.3 %collective-permute-done.15 = f32[32,16,1]{2,1,0:T(8,128)S(1)} collective-permute-done((f32[32,16,1]{2,1,0:T(8,128)S(1)}, f32[32,16,1]{2,1,0:T(8,128)S(1)}, u32[]{:S(2)}, u32[]{:S(2)}) %collective-permute-start.15) | collective-permute-done | bytes 2080 | tf_op jit(solution)/shard_map/ppermute | solution.py:26
  162.2 1.3 collective-permute-start.16
  163.5 4.9 %collective-permute-start.17 = (f32[32,1,130]{2,1,0:T(1,128)S(1)}, f32[32,1,130]{2,1,0:T(1,128)S(1)}, u32[]{:S(2)}, u32[]{:S(2)}) collective-permute-start(f32[32,1,130]{2,1,0:T(1,128)S(1)} %get-tuple-element.43), channel_id=1, source_target_pairs={{0,1},{1,2},{2,3},{4,5},{5,6},{6,7},{8,9},{9,10},{10,11},{12,13},{... | collective-permute-start | bytes 49928 | tf_op jit(solution)/shard_map/ppermute | solution.py:26
  168.4 1.5 collective-permute-done.17
  169.9 2.2 %fusion.73 = (f32[]{:T(128)}, f32[]{:T(128)}, f32[32,16,128]{2,1,0:T(8,128)}) fusion(f32[4,8,16,128]{3,2,1,0:T(8,128)S(1)} %all_to_all.41, f32[32,16,128]{2,1,0:T(8,128)S(1)} %copy-done.8, f32[32,16,128]{2,1,0:T(8,128)S(1)} %fusion.31, f32[31,16,128]{2,1,0:T(8,128)S(1)} %get-tuple-element.63, f32[31,16,128]{2,1,0:T(8,128)S(1)} %slice.350, ...), kind=kLoop, calls=%fused_computation.132 | loop fusion | flops 2359294 | bytes 3682824 | tf_op jit(solution)/shard_map/reduce_sum | solution.py:145
  172.2 32.6 %all-reduce.11 = (f32[]{:T(128)}, f32[]{:T(128)}) all-reduce(f32[]{:T(128)} %get-tuple-element.29, f32[]{:T(128)} %get-tuple-element.28), channel_id=1, replica_groups=mesh['ens'=2,'lon'=4,'lat'=4] {'lon','lat'}, use_global_device_ids=true, to_apply=%region_5.6 | all-reduce | flops 2 | bytes 16 | tf_op jit(solution)/shard_map/psum | solution.py:145
  209.3 1.9 multiply_subtract_fusion
  (108 shorter events, 33.3 us)
Async XLA Ops:
  0.6 6.3 %copy-start.11 = (f32[3,32,16,128]{3,2,1,0:T(8,128)S(1)}, f32[3,32,16,128]{3,2,1,0:T(8,128)}, u32[]{:S(2)}) copy-start(f32[3,32,16,128]{3,2,1,0:T(8,128)} %param.10) | copy-start | bytes 2359300
  0.6 19.3 %all-to-all-start = ((f32[32,16,128]{2,1,0:T(8,128)}), f32[32,16,128]{2,1,0:T(8,128)S(1)}, u32[]{:S(2)}, u32[]{:S(2)}) async-start(f32[32,16,128]{2,1,0:T(8,128)} %param.8), calls=%async_computation | async-start | bytes 524288 | tf_op jit(solution)/shard_map/all_to_all | solution.py:139
  7.2 6.7 %collective-permute-start = (f32[32,16,1]{2,1,0:T(8,128)S(1)}, f32[32,16,1]{2,1,0:T(8,128)S(1)}, u32[]{:S(2)}, u32[]{:S(2)}) collective-permute-start(f32[32,16,1]{2,1,0:T(8,128)S(1)} %slice.335), channel_id=1, source_target_pairs={{0,4},{4,8},{8,12},{12,0},{1,5},{5,9},{9,13},{13,1},{2,6},{6,10},{... | collective-permute-start | bytes 6152 | tf_op jit(solution)/shard_map/ppermute | solution.py:34
  8.0 6.0 %copy-start.1 = (f32[5,32,16,128]{3,2,1,0:T(8,128)}, f32[5,32,16,128]{3,2,1,0:T(8,128)S(1)}, u32[]{:S(2)}) copy-start(f32[5,32,16,128]{3,2,1,0:T(8,128)S(1)} %select_dynamic-update-slice_fusion) | copy-start | bytes 3932164
  14.2 1.3 copy-start.2
  15.9 16.5 %collective-permute-start.1 = (f32[32,1,130]{2,1,0:T(1,128)S(1)}, f32[32,1,130]{2,1,0:T(1,128)S(1)}, u32[]{:S(2)}, u32[]{:S(2)}) collective-permute-start(f32[32,1,130]{2,1,0:T(1,128)S(1)} %slice.336), channel_id=1, source_target_pairs={{0,1},{1,2},{2,3},{4,5},{5,6},{6,7},{8,9},{9,10},{10,11},{12,13},{... | collective-permute-start | bytes 49928 | tf_op jit(solution)/shard_map/ppermute | solution.py:40
  28.9 9.4 %all-to-all-start.1 = ((f32[4,8,16,128]{3,2,1,0:T(8,128)}), f32[4,8,16,128]{3,2,1,0:T(8,128)S(1)}, u32[]{:S(2)}, u32[]{:S(2)}) async-start(f32[4,8,16,128]{3,2,1,0:T(8,128)} %pad_maximum_fusion.34), calls=%async_computation.1 | async-start | bytes 524288 | tf_op jit(solution)/shard_map/all_to_all | solution.py:15
  32.4 6.0 %copy-start = (s32[32,16,128]{2,1,0:T(8,128)S(1)}, s32[32,16,128]{2,1,0:T(8,128)}, u32[]{:S(2)}) copy-start(s32[32,16,128]{2,1,0:T(8,128)} %param.11) | copy-start | bytes 786436
  38.3 0.7 copy-start.5
  38.5 7.5 %collective-permute-start.3 = (f32[32,16,1]{2,1,0:T(8,128)S(1)}, f32[32,16,1]{2,1,0:T(8,128)S(1)}, u32[]{:S(2)}, u32[]{:S(2)}) collective-permute-start(f32[32,16,1]{2,1,0:T(8,128)S(1)} %get-tuple-element.78), channel_id=1, source_target_pairs={{0,4},{4,8},{8,12},{12,0},{1,5},{5,9},{9,13},{13,1},{2,6},{6,10},{... | collective-permute-start | bytes 6152 | tf_op jit(solution)/shard_map/ppermute | solution.py:26
  39.0 7.0 %collective-permute-start.2 = (f32[32,16,1]{2,1,0:T(8,128)S(1)}, f32[32,16,1]{2,1,0:T(8,128)S(1)}, u32[]{:S(2)}, u32[]{:S(2)}) collective-permute-start(f32[32,16,1]{2,1,0:T(8,128)S(1)} %get-tuple-element.79), channel_id=1, source_target_pairs={{4,0},{8,4},{12,8},{0,12},{5,1},{9,5},{13,9},{1,13},{6,2},{10,6},{... | collective-permute-start | bytes 6152 | tf_op jit(solution)/shard_map/ppermute | solution.py:27
  42.5 28.1 %copy-start.3 = (f32[32,18,130]{2,1,0:T(8,128)}, f32[32,18,130]{2,1,0:T(8,128)S(1)}, u32[]{:S(2)}) copy-start(f32[32,18,130]{2,1,0:T(8,128)S(1)} %get-tuple-element.38) | copy-start | bytes 898564
  46.3 6.1 %collective-permute-start.4 = (f32[32,1,130]{2,1,0:T(1,128)S(1)}, f32[32,1,130]{2,1,0:T(1,128)S(1)}, u32[]{:S(2)}, u32[]{:S(2)}) collective-permute-start(f32[32,1,130]{2,1,0:T(1,128)S(1)} %get-tuple-element.50), channel_id=1, source_target_pairs={{1,0},{2,1},{3,2},{5,4},{6,5},{7,6},{9,8},{10,9},{11,10},{13,12},{... | collective-permute-start | bytes 49928 | tf_op jit(solution)/shard_map/ppermute | solution.py:27
  47.6 6.1 %collective-permute-start.5 = (f32[32,1,130]{2,1,0:T(1,128)S(1)}, f32[32,1,130]{2,1,0:T(1,128)S(1)}, u32[]{:S(2)}, u32[]{:S(2)}) collective-permute-start(f32[32,1,130]{2,1,0:T(1,128)S(1)} %get-tuple-element.51), channel_id=1, source_target_pairs={{0,1},{1,2},{2,3},{4,5},{5,6},{6,7},{8,9},{9,10},{10,11},{12,13},{... | collective-permute-start | bytes 49928 | tf_op jit(solution)/shard_map/ppermute | solution.py:26
  54.6 15.9 %copy-start.6 = (f32[4,8,16,128]{3,2,1,0:T(8,128)S(1)}, f32[4,8,16,128]{3,2,1,0:T(8,128)}, u32[]{:S(2)}) copy-start(f32[4,8,16,128]{3,2,1,0:T(8,128)} %copy-done.5) | copy-start | bytes 786436
  54.6 15.9 %copy-start.10 = (f32[32,16,128]{2,1,0:T(8,128)S(1)}, f32[32,16,128]{2,1,0:T(8,128)}, u32[]{:S(2)}) copy-start(f32[32,16,128]{2,1,0:T(8,128)} %param.8) | copy-start | bytes 786436
  54.8 7.5 %collective-permute-start.7 = (f32[32,16,1]{2,1,0:T(8,128)S(1)}, f32[32,16,1]{2,1,0:T(8,128)S(1)}, u32[]{:S(2)}, u32[]{:S(2)}) collective-permute-start(f32[32,16,1]{2,1,0:T(8,128)S(1)} %get-tuple-element.72), channel_id=1, source_target_pairs={{0,4},{4,8},{8,12},{12,0},{1,5},{5,9},{9,13},{13,1},{2,6},{6,10},{... | collective-permute-start | bytes 6152 | tf_op jit(solution)/shard_map/ppermute | solution.py:26
  54.8 7.5 %collective-permute-start.6 = (f32[32,16,1]{2,1,0:T(8,128)S(1)}, f32[32,16,1]{2,1,0:T(8,128)S(1)}, u32[]{:S(2)}, u32[]{:S(2)}) collective-permute-start(f32[32,16,1]{2,1,0:T(8,128)S(1)} %get-tuple-element.73), channel_id=1, source_target_pairs={{4,0},{8,4},{12,8},{0,12},{5,1},{9,5},{13,9},{1,13},{6,2},{10,6},{... | collective-permute-start | bytes 6152 | tf_op jit(solution)/shard_map/ppermute | solution.py:27
  62.6 6.2 %collective-permute-start.8 = (f32[32,1,130]{2,1,0:T(1,128)S(1)}, f32[32,1,130]{2,1,0:T(1,128)S(1)}, u32[]{:S(2)}, u32[]{:S(2)}) collective-permute-start(f32[32,1,130]{2,1,0:T(1,128)S(1)} %get-tuple-element.46), channel_id=1, source_target_pairs={{1,0},{2,1},{3,2},{5,4},{6,5},{7,6},{9,8},{10,9},{11,10},{13,12},{... | collective-permute-start | bytes 49928 | tf_op jit(solution)/shard_map/ppermute | solution.py:27
  63.9 6.6 %collective-permute-start.9 = (f32[32,1,130]{2,1,0:T(1,128)S(1)}, f32[32,1,130]{2,1,0:T(1,128)S(1)}, u32[]{:S(2)}, u32[]{:S(2)}) collective-permute-start(f32[32,1,130]{2,1,0:T(1,128)S(1)} %get-tuple-element.47), channel_id=1, source_target_pairs={{0,1},{1,2},{2,3},{4,5},{5,6},{6,7},{8,9},{9,10},{10,11},{12,13},{... | collective-permute-start | bytes 49928 | tf_op jit(solution)/shard_map/ppermute | solution.py:26
  72.1 48.3 %copy-start.9 = (f32[32,16,128]{2,1,0:T(8,128)}, f32[32,16,128]{2,1,0:T(8,128)S(1)}, u32[]{:S(2)}) copy-start(f32[32,16,128]{2,1,0:T(8,128)S(1)} %get-tuple-element.37) | copy-start | bytes 786436
  109.4 0.7 copy-start.7
  136.9 15.8 %copy-start.4 = (f32[32,18,130]{2,1,0:T(8,128)S(1)}, f32[32,18,130]{2,1,0:T(8,128)}, u32[]{:S(2)}) copy-start(f32[32,18,130]{2,1,0:T(8,128)} %copy-done.3) | copy-start | bytes 898564
  137.0 8.0 %collective-permute-start.11 = (f32[32,16,1]{2,1,0:T(8,128)S(1)}, f32[32,16,1]{2,1,0:T(8,128)S(1)}, u32[]{:S(2)}, u32[]{:S(2)}) collective-permute-start(f32[32,16,1]{2,1,0:T(8,128)S(1)} %get-tuple-element.66), channel_id=1, source_target_pairs={{0,4},{4,8},{8,12},{12,0},{1,5},{5,9},{9,13},{13,1},{2,6},{6,10},{... | collective-permute-start | bytes 6152 | tf_op jit(solution)/shard_map/ppermute | solution.py:26
  137.1 7.9 %collective-permute-start.10 = (f32[32,16,1]{2,1,0:T(8,128)S(1)}, f32[32,16,1]{2,1,0:T(8,128)S(1)}, u32[]{:S(2)}, u32[]{:S(2)}) collective-permute-start(f32[32,16,1]{2,1,0:T(8,128)S(1)} %get-tuple-element.67), channel_id=1, source_target_pairs={{4,0},{8,4},{12,8},{0,12},{5,1},{9,5},{13,9},{1,13},{6,2},{10,6},{... | collective-permute-start | bytes 6152 | tf_op jit(solution)/shard_map/ppermute | solution.py:27
  145.3 5.9 %collective-permute-start.12 = (f32[32,1,130]{2,1,0:T(1,128)S(1)}, f32[32,1,130]{2,1,0:T(1,128)S(1)}, u32[]{:S(2)}, u32[]{:S(2)}) collective-permute-start(f32[32,1,130]{2,1,0:T(1,128)S(1)} %get-tuple-element.44), channel_id=1, source_target_pairs={{1,0},{2,1},{3,2},{5,4},{6,5},{7,6},{9,8},{10,9},{11,10},{13,12},{... | collective-permute-start | bytes 49928 | tf_op jit(solution)/shard_map/ppermute | solution.py:27
  146.6 6.1 %collective-permute-start.13 = (f32[32,1,130]{2,1,0:T(1,128)S(1)}, f32[32,1,130]{2,1,0:T(1,128)S(1)}, u32[]{:S(2)}, u32[]{:S(2)}) collective-permute-start(f32[32,1,130]{2,1,0:T(1,128)S(1)} %get-tuple-element.45), channel_id=1, source_target_pairs={{0,1},{1,2},{2,3},{4,5},{5,6},{6,7},{8,9},{9,10},{10,11},{12,13},{... | collective-permute-start | bytes 49928 | tf_op jit(solution)/shard_map/ppermute | solution.py:26
  153.6 16.3 %copy-start.8 = (f32[32,16,128]{2,1,0:T(8,128)S(1)}, f32[32,16,128]{2,1,0:T(8,128)}, u32[]{:S(2)}) copy-start(f32[32,16,128]{2,1,0:T(8,128)} %copy-done.7) | copy-start | bytes 786436
  153.8 8.1 %collective-permute-start.15 = (f32[32,16,1]{2,1,0:T(8,128)S(1)}, f32[32,16,1]{2,1,0:T(8,128)S(1)}, u32[]{:S(2)}, u32[]{:S(2)}) collective-permute-start(f32[32,16,1]{2,1,0:T(8,128)S(1)} %get-tuple-element.60), channel_id=1, source_target_pairs={{0,4},{4,8},{8,12},{12,0},{1,5},{5,9},{9,13},{13,1},{2,6},{6,10},{... | collective-permute-start | bytes 6152 | tf_op jit(solution)/shard_map/ppermute | solution.py:26
  153.9 8.1 %collective-permute-start.14 = (f32[32,16,1]{2,1,0:T(8,128)S(1)}, f32[32,16,1]{2,1,0:T(8,128)S(1)}, u32[]{:S(2)}, u32[]{:S(2)}) collective-permute-start(f32[32,16,1]{2,1,0:T(8,128)S(1)} %get-tuple-element.61), channel_id=1, source_target_pairs={{4,0},{8,4},{12,8},{0,12},{5,1},{9,5},{13,9},{1,13},{6,2},{10,6},{... | collective-permute-start | bytes 6152 | tf_op jit(solution)/shard_map/ppermute | solution.py:27
  162.2 6.2 %collective-permute-start.16 = (f32[32,1,130]{2,1,0:T(1,128)S(1)}, f32[32,1,130]{2,1,0:T(1,128)S(1)}, u32[]{:S(2)}, u32[]{:S(2)}) collective-permute-start(f32[32,1,130]{2,1,0:T(1,128)S(1)} %get-tuple-element.42), channel_id=1, source_target_pairs={{1,0},{2,1},{3,2},{5,4},{6,5},{7,6},{9,8},{10,9},{11,10},{13,12},{... | collective-permute-start | bytes 49928 | tf_op jit(solution)/shard_map/ppermute | solution.py:27
  163.5 6.4 %collective-permute-start.17 = (f32[32,1,130]{2,1,0:T(1,128)S(1)}, f32[32,1,130]{2,1,0:T(1,128)S(1)}, u32[]{:S(2)}, u32[]{:S(2)}) collective-permute-start(f32[32,1,130]{2,1,0:T(1,128)S(1)} %get-tuple-element.43), channel_id=1, source_target_pairs={{0,1},{1,2},{2,3},{4,5},{5,6},{6,7},{8,9},{9,10},{10,11},{12,13},{... | collective-permute-start | bytes 49928 | tf_op jit(solution)/shard_map/ppermute | solution.py:26
